TPU v7x, 128 devices: a whole 4x4x4 slice. The times are simulated.
128 devices in a mesh: lat: 16 (over y, z), lon: 8 (over x, core).
Axes of the slice: x: 4, y: 4, z: 4, core: 2. Of those that a mesh axis runs over, the one named last changes fastest.
Arguments:
- inputs: bfloat16 [640, 1440, 256], P('lat', 'lon'), may hold values from -6 to 6
- w_enc: bfloat16 [3, 3, 256, 256], replicated, may hold values from -0.125 to 0.125
- w_proj: bfloat16 [256, 128], replicated, may hold values from -0.375 to 0.375
- film_scale: float32 [720, 128], replicated, may hold values from -3 to 3
- film_shift: float32 [720, 128], replicated, may hold values from -3 to 3
- lead_ids: int32 [16], replicated, may hold values from 0 to 719
- w_head: bfloat16 [3, 3, 128, 128], replicated, may hold values from -0.1875 to 0.1875
- zonal_mix: bfloat16 [720, 720], replicated, may hold values from -0.21875 to 0.21875
Outputs:
- forecast: bfloat16 [16, 320, 720, 128], P('lon', 'lat')
Inputs may be any that keep to these rules, and one draw needn't show every extreme that they name: `lead_ids`: rows of the tables; repeats may occur.
All inputs are finite; a program needn't handle non-finite values.
Results may differ from a plain program's by a relative error of at most 0.015.
Values may be sent and summed in bfloat16 or wider, within the bound.
A program may use at most 128 MiB of HBM per device.

v0:
```python
import jax
import jax.numpy as jnp
from jax import lax
from jax.sharding import PartitionSpec as P

LEAD_DEV = 2


def extended(x, sides, width, wrap):
    for axis, dim in sides:
        devices, length = (lax.axis_size(axis), x.shape[dim])
        up = [(i, (i + 1) % devices) for i in range(devices if wrap else devices - 1)]
        down = [(j, i) for i, j in up]
        last = lax.slice_in_dim(x, length - width, length, axis=dim)
        initial = lax.slice_in_dim(x, 0, width, axis=dim)
        before = lax.ppermute(last, axis, up)
        after = lax.ppermute(initial, axis, down)
        x = jnp.concatenate([before, x, after], axis=dim)
    return x


def conv_three(padded, weight):
    batched = padded if padded.ndim == 4 else padded[None]
    result = lax.conv_general_dilated(
        batched,
        weight,
        (1, 1),
        "VALID",
        dimension_numbers=("NHWC", "HWIO", "NHWC"),
        preferred_element_type=jnp.float32,
    )
    return result if padded.ndim == 4 else result[0]


def pool_pairs(field):
    summed = lax.reduce_window(
        field, jnp.array(0, field.dtype), lax.add, (2, 2, 1), (2, 2, 1), "VALID"
    )
    return summed * 0.25


def wrap_columns(field):
    return jnp.concatenate([field[..., -1:, :], field, field[..., :1, :]], axis=-2)


def modulate(projected, scales, shifts):
    widened = projected.astype(jnp.float32)[None]
    return (widened * (1.0 + scales[:, None, None, :]) + shifts[:, None, None, :]).astype(
        jnp.bfloat16
    )


def shards(inputs, w_enc, w_proj, film_scale, film_shift, lead_ids, w_head, zonal_mix):
    lat_rows, lon_cols, channels = inputs.shape
    with_rows = extended(inputs, (("lat", 0),), 1, False)
    padded = extended(with_rows, (("lon", 1),), 1, True)
    encoded = jax.nn.gelu(conv_three(padded, w_enc))
    pooled = pool_pairs(encoded).astype(jnp.bfloat16)
    head_width = w_proj.shape[1]
    lon_group = lax.axis_index("lon")
    my_rows = lax.dynamic_slice_in_dim(lead_ids, lon_group * LEAD_DEV, LEAD_DEV)
    flat = jnp.dot(pooled.reshape(-1, channels), w_proj, preferred_element_type=jnp.float32)
    band_proj = lax.all_gather(
        flat.astype(jnp.bfloat16).reshape(pooled.shape[0], pooled.shape[1], head_width),
        "lon",
        axis=1,
        tiled=True,
    )
    onehot = (my_rows[:, None] == jnp.arange(film_scale.shape[0], dtype=jnp.int32)[None, :]).astype(
        jnp.float32
    )
    scales = jnp.dot(onehot, film_scale, precision=lax.Precision.HIGHEST)
    shifts = jnp.dot(onehot, film_shift, precision=lax.Precision.HIGHEST)
    scales, shifts = (scales, shifts)
    with_band = None
    modulated = modulate(band_proj, scales, shifts)
    with_band = extended(modulated, (("lat", 1),), 1, False)
    padded_head = wrap_columns(with_band)
    hidden = jax.nn.gelu(conv_three(padded_head, w_head)).astype(jnp.bfloat16)
    mixed = jnp.einsum("ij,bajc->baic", zonal_mix, hidden, preferred_element_type=jnp.float32)
    return (modulated.astype(jnp.float32) + mixed).astype(jnp.bfloat16)


def solution(mesh):
    in_specs = (P("lat", "lon", None), P(), P(), P(), P(), P(), P(), P())
    out_specs = P("lon", "lat", None, None)
    return jax.shard_map(shards, mesh=mesh, in_specs=in_specs, out_specs=out_specs, check_vma=False)
```

profile of v0, /device:TPU:96, one launch (start us, length us, event | category | flops | bytes accessed | tf_op | source)
XLA Modules:
  0.0 219.7 jit_solution(3243540371353144879)
XLA Ops:
  6.5 1.8 fusion.43
  8.4 2.4 %collective-permute-start.1 = (bf16[1,180,256]{2,1,0:T(8,128)(2,1)S(1)}, bf16[1,180,256]{2,1,0:T(8,128)(2,1)S(1)}, u32[]{:S(2)}, u32[]{:S(2)}) collective-permute-start(bf16[1,180,256]{2,1,0:T(8,128)(2,1)S(1)} %copy.64), channel_id=1, source_target_pairs={{8,0},{16,8},{24,16},{32,24},{40,32},{48,40},{56,48},{64,56},{72,6... | collective-permute-start | bytes 276488 | tf_op jit(solution)/shard_map/ppermute | solution.py:17
  10.8 5.6 %collective-permute-start = (bf16[1,180,256]{2,1,0:T(8,128)(2,1)S(1)}, bf16[1,180,256]{2,1,0:T(8,128)(2,1)S(1)}, u32[]{:S(2)}, u32[]{:S(2)}) collective-permute-start(bf16[1,180,256]{2,1,0:T(8,128)(2,1)S(1)} %copy.63), channel_id=1, source_target_pairs={{0,8},{8,16},{16,24},{24,32},{32,40},{40,48},{48,56},{56,64},{64,7... | collective-permute-start | bytes 276488 | tf_op jit(solution)/shard_map/ppermute | solution.py:16
  19.6 2.9 %collective-permute-start.3 = (bf16[42,1,256]{2,0,1:T(8,128)(2,1)S(1)}, bf16[42,1,256]{2,0,1:T(8,128)(2,1)S(1)}, u32[]{:S(2)}, u32[]{:S(2)}) collective-permute-start(bf16[42,1,256]{2,0,1:T(8,128)(2,1)S(1)} %get-tuple-element.8), channel_id=1, source_target_pairs={{1,0},{2,1},{3,2},{4,3},{5,4},{6,5},{7,6},{0,7},{9,8},{10,9},{11,1... | collective-permute-start | bytes 64520 | tf_op jit(solution)/shard_map/ppermute | solution.py:17
  24.0 3.2 %maximum_bitcast_fusion = bf16[42,1,182,256]{3,0,2,1:T(8,128)(2,1)S(1)} fusion(bf16[42,1,256]{2,0,1:T(8,128)(2,1)S(1)} %collective-permute-done.3, bf16[1,180,256]{2,0,1:T(2,128)(2,1)S(1)} %copy.46, bf16[40,180,256]{2,0,1:T(8,128)(2,1)S(1)} %copy-done.2, bf16[1,180,256]{2,0,1:T(2,128)(2,1)S(1)} %copy.45, bf16[42,1,256]{2,0,1:T(8,128)(2,1)S(1)} %collective-permute-done.2), kind=kLoop, calls=%fused_computation.37 | loop fusion | flops 19568640 | bytes 7827456 | tf_op jit(solution)/shard_map/broadcast_in_dim | solution.py:23
  29.2 9.5 %broadcast_select_fusion = f32[40,8,23,256]{3,1,2,0:T(8,128)S(1)} fusion(pred[8,23]{0,1:T(8,128)(4,1)S(1)} %copy-done.9, bf16[3,3,256,256]{3,2,1,0:T(8,128)(2,1)S(1)} %copy-done, bf16[42,1,7,2,256]{4,2,3,0,1:T(8,128)(2,1)S(1)} %slice.36, bf16[42,1,8,23,256]{4,2,3,0,1:T(8,128)(2,1)S(1)} %copy.49), kind=kOutput, calls=%fused_computation.44 | convolution fusion | flops 8696995840 | bytes 12974264 | tf_op jit(solution)/shard_map/conv_general_dilated | solution.py:24
  38.8 2.6 %copy.50 = f32[40,8,23,256]{3,0,2,1:T(8,128)S(1)} copy(f32[40,8,23,256]{3,1,2,0:T(8,128)S(1)} %broadcast_select_fusion) | data formatting | bytes 15073280 | tf_op jit(solution)/shard_map/conv_general_dilated | solution.py:24
  41.4 4.2 %fusion.23 = f32[40,180,256]{2,0,1:T(8,128)} fusion(f32[40,1,184,256]{3,0,2,1:T(8,128)S(1)} %bitcast.42), kind=kLoop, calls=%fused_computation.33 | loop fusion | flops 14745600 | bytes 14745600 | tf_op jit(solution)/shard_map/mul | solution.py:57
  45.5 8.4 %reduce_window.7 = f32[20,90,256]{2,0,1:T(8,128)S(1)} reduce-window(f32[40,180,256]{2,0,1:T(8,128)} %fusion.23, f32[]{:T(128)} %constant.14.clone.1), window={size=2x2x1 stride=2x2x1}, to_apply=%region_0.0 | reduce-window | flops 1382400 | bytes 9216004 | tf_op jit(solution)/shard_map/reduce_window | solution.py:36
  57.8 33.8 %all-gather.2.cloned.1.call-done = bf16[20,720,128]{2,0,1:T(8,128)(2,1)} async-done(((bf16[20,90,128]{2,0,1:T(8,128)(2,1)}), bf16[20,720,128]{2,0,1:T(8,128)(2,1)}) %all-gather.2.cloned.1.call-update) | async-done | bytes 3686416 | tf_op jit(solution)/shard_map/all_gather | solution.py:63
  91.5 5.8 %copy_convert_fusion = f32[20,720,128]{2,1,0:T(8,128)} fusion(bf16[20,720,128]{2,0,1:T(8,128)(2,1)} %all-gather.2.cloned.1.call-done), kind=kLoop, calls=%fused_computation.45 | loop fusion | flops 1843200 | bytes 11059200 | tf_op jit(solution)/shard_map/convert_element_type | solution.py:47
  97.3 7.6 %add_convert_fusion = bf16[2,20,720,128]{3,2,1,0:T(8,128)(2,1)} fusion(f32[2,128]{1,0:T(2,128)S(1)} %fusion.36, f32[2,128]{1,0:T(2,128)S(1)} %convolution_add_fusion, f32[20,720,128]{2,1,0:T(8,128)} %copy_convert_fusion), kind=kLoop, calls=%fused_computation.13 | loop fusion | flops 11059200 | bytes 14747648 | tf_op jit(solution)/shard_map/convert_element_type | solution.py:48
  106.1 3.1 %collective-permute-start.4 = (bf16[2,1,720,128]{3,2,1,0:T(8,128)(2,1)S(1)}, bf16[2,1,720,128]{3,2,1,0:T(8,128)(2,1)S(1)}, u32[]{:S(2)}, u32[]{:S(2)}) collective-permute-start(bf16[2,1,720,128]{3,2,1,0:T(8,128)(2,1)S(1)} %get-tuple-element.5), channel_id=1, source_target_pairs={{0,8},{8,16},{16,24},{24,32},{32,40},{40,48},{48,56},{56,64},{64,7... | collective-permute-start | bytes 1105928 | tf_op jit(solution)/shard_map/ppermute | solution.py:16
  109.3 2.7 %collective-permute-start.5 = (bf16[2,1,720,128]{3,2,1,0:T(8,128)(2,1)S(1)}, bf16[2,1,720,128]{3,2,1,0:T(8,128)(2,1)S(1)}, u32[]{:S(2)}, u32[]{:S(2)}) collective-permute-start(bf16[2,1,720,128]{3,2,1,0:T(8,128)(2,1)S(1)} %get-tuple-element.6), channel_id=1, source_target_pairs={{8,0},{16,8},{24,16},{32,24},{40,32},{48,40},{56,48},{64,56},{72,6... | collective-permute-start | bytes 1105928 | tf_op jit(solution)/shard_map/ppermute | solution.py:17
  112.0 6.8 %collective-permute-done.4 = bf16[2,1,720,128]{3,2,1,0:T(8,128)(2,1)S(1)} collective-permute-done((bf16[2,1,720,128]{3,2,1,0:T(8,128)(2,1)S(1)}, bf16[2,1,720,128]{3,2,1,0:T(8,128)(2,1)S(1)}, u32[]{:S(2)}, u32[]{:S(2)}) %collective-permute-start.4) | collective-permute-done | bytes 368672 | tf_op jit(solution)/shard_map/ppermute | solution.py:16
  118.8 5.0 %collective-permute-done.5 = bf16[2,1,720,128]{3,2,1,0:T(8,128)(2,1)S(1)} collective-permute-done((bf16[2,1,720,128]{3,2,1,0:T(8,128)(2,1)S(1)}, bf16[2,1,720,128]{3,2,1,0:T(8,128)(2,1)S(1)}, u32[]{:S(2)}, u32[]{:S(2)}) %collective-permute-start.5) | collective-permute-done | bytes 368672 | tf_op jit(solution)/shard_map/ppermute | solution.py:17
  123.7 13.0 %fusion.15 = bf16[22,2,722,128]{3,2,0,1:T(8,128)(2,1)} fusion(bf16[2,1,720,128]{3,2,1,0:T(8,128)(2,1)S(1)} %collective-permute-done.5, bf16[2,20,720,128]{3,2,1,0:T(8,128)(2,1)} %add_convert_fusion, bf16[2,1,720,128]{3,2,1,0:T(8,128)(2,1)S(1)} %collective-permute-done.4), kind=kLoop, calls=%fused_computation.22 | loop fusion | flops 73193472 | bytes 16242688 | tf_op jit(solution)/shard_map/concatenate | solution.py:43
  136.8 7.0 %pad.2 = bf16[22,2,728,128]{3,2,0,1:T(8,128)(2,1)} pad(bf16[22,2,722,128]{3,2,0,1:T(8,128)(2,1)} %fusion.15, bf16[]{:T(256)} %constant.6), padding=0_0x0_0x0_6x0_0 | pad | bytes 16332802 | tf_op jit(solution)/shard_map/concatenate | solution.py:43
  143.8 12.6 %reshape.39 = bf16[22,2,8,91,128]{4,3,2,0,1:T(8,128)(2,1)} reshape(bf16[22,2,728,128]{3,2,0,1:T(8,128)(2,1)} %pad.2) | data formatting | bytes 16400384 | tf_op jit(solution)/shard_map/conv_general_dilated | solution.py:24
  157.7 4.6 %fusion.10 = bf16[22,2,8,93,128]{4,3,2,1,0:T(8,128)(2,1)S(1)} fusion(bf16[22,2,7,2,128]{4,3,2,1,0:T(2,128)(2,1)S(1)} %copy.77, bf16[22,2,8,91,128]{4,3,2,0,1:T(8,128)(2,1)} %reshape.39), kind=kLoop, calls=%fused_computation.15 | loop fusion | flops 25141248 | bytes 16738304 | tf_op jit(solution)/shard_map/conv_general_dilated | solution.py:24
  162.3 21.3 %fusion.8 = bf16[20,16,91,128]{3,1,2,0:T(8,128)(2,1)S(1)} fusion(bf16[3,3,128,128]{3,2,1,0:T(8,128)(2,1)S(1)} %copy-done.6, bf16[22,2,8,93,128]{4,3,2,1,0:T(8,128)(2,1)S(1)} %fusion.10, pred[16,91]{0,1:T(8,128)(4,1)S(1)} %copy-done.8), kind=kOutput, calls=%fused_computation.10 | convolution fusion | flops 8625111040 | bytes 16131504 | tf_op jit(solution)/shard_map/conv_general_dilated | solution.py:24
  183.6 5.1 %copy.56 = bf16[20,16,91,128]{3,2,1,0:T(8,128)(2,1)} copy(bf16[20,16,91,128]{3,1,2,0:T(8,128)(2,1)S(1)} %fusion.8) | data formatting | bytes 14909440 | tf_op jit(solution)/shard_map/convert_element_type | solution.py:79
  188.7 11.6 %reshape.27 = bf16[20,2,728,128]{3,2,1,0:T(8,128)(2,1)} reshape(bf16[20,16,91,128]{3,2,1,0:T(8,128)(2,1)} %copy.56) | data formatting | bytes 14909440 | tf_op jit(solution)/shard_map/convert_element_type | solution.py:79
  200.3 12.3 %fusion.9 = bf16[2,20,720,128]{3,2,1,0:T(8,128)(2,1)} fusion(bf16[2,20,720,128]{3,2,1,0:T(8,128)(2,1)} %add_convert_fusion, bf16[720,720]{1,0:T(8,128)(2,1)S(1)} %copy-done.5, bf16[20,2,728,128]{3,2,1,0:T(8,128)(2,1)} %reshape.27), kind=kOutput, calls=%fused_computation.12 | convolution fusion | flops 5319475200 | bytes 23155200 | tf_op jit(solution)/shard_map/ij,bajc->baic/dot_general | solution.py:80
  (47 shorter events, 12.8 us)
Async XLA Ops:
  6.5 22.7 %copy-start = (bf16[3,3,256,256]{3,2,1,0:T(8,128)(2,1)S(1)}, bf16[3,3,256,256]{3,2,1,0:T(8,128)(2,1)}, u32[]{:S(2)}) copy-start(bf16[3,3,256,256]{3,2,1,0:T(8,128)(2,1)} %param.9) | copy-start | bytes 3538948
  6.5 85.0 %all-gather.2.cloned.1.call-start = ((), (), s32[]{:S(2)}) async-start(), calls=%async_computation | async-start | bytes 4976640 | tf_op jit(solution)/shard_map/all_gather | solution.py:63
  6.5 17.5 %copy-start.2 = (bf16[40,180,256]{2,0,1:T(8,128)(2,1)S(1)}, bf16[40,180,256]{2,0,1:T(8,128)(2,1)}, u32[]{:S(2)}) copy-start(bf16[40,180,256]{2,0,1:T(8,128)(2,1)} %param.8) | copy-start | bytes 11059204
  8.4 8.7 %collective-permute-start.1 = (bf16[1,180,256]{2,1,0:T(8,128)(2,1)S(1)}, bf16[1,180,256]{2,1,0:T(8,128)(2,1)S(1)}, u32[]{:S(2)}, u32[]{:S(2)}) collective-permute-start(bf16[1,180,256]{2,1,0:T(8,128)(2,1)S(1)} %copy.64), channel_id=1, source_target_pairs={{8,0},{16,8},{24,16},{32,24},{40,32},{48,40},{56,48},{64,56},{72,6... | collective-permute-start | bytes 276488 | tf_op jit(solution)/shard_map/ppermute | solution.py:17
  10.8 7.8 %collective-permute-start = (bf16[1,180,256]{2,1,0:T(8,128)(2,1)S(1)}, bf16[1,180,256]{2,1,0:T(8,128)(2,1)S(1)}, u32[]{:S(2)}, u32[]{:S(2)}) collective-permute-start(bf16[1,180,256]{2,1,0:T(8,128)(2,1)S(1)} %copy.63), channel_id=1, source_target_pairs={{0,8},{8,16},{16,24},{24,32},{32,40},{40,48},{48,56},{56,64},{64,7... | collective-permute-start | bytes 276488 | tf_op jit(solution)/shard_map/ppermute | solution.py:16
  19.5 4.5 %collective-permute-start.2 = (bf16[42,1,256]{2,0,1:T(8,128)(2,1)S(1)}, bf16[42,1,256]{2,0,1:T(8,128)(2,1)S(1)}, u32[]{:S(2)}, u32[]{:S(2)}) collective-permute-start(bf16[42,1,256]{2,0,1:T(8,128)(2,1)S(1)} %get-tuple-element.7), channel_id=1, source_target_pairs={{0,1},{1,2},{2,3},{3,4},{4,5},{5,6},{6,7},{7,0},{8,9},{9,10},{10,1... | collective-permute-start | bytes 64520 | tf_op jit(solution)/shard_map/ppermute | solution.py:16
  19.6 4.5 %collective-permute-start.3 = (bf16[42,1,256]{2,0,1:T(8,128)(2,1)S(1)}, bf16[42,1,256]{2,0,1:T(8,128)(2,1)S(1)}, u32[]{:S(2)}, u32[]{:S(2)}) collective-permute-start(bf16[42,1,256]{2,0,1:T(8,128)(2,1)S(1)} %get-tuple-element.8), channel_id=1, source_target_pairs={{1,0},{2,1},{3,2},{4,3},{5,4},{6,5},{7,6},{0,7},{9,8},{10,9},{11,1... | collective-permute-start | bytes 64520 | tf_op jit(solution)/shard_map/ppermute | solution.py:17
  27.2 2.0 copy-start.9
  45.5 9.1 %copy-start.4 = (bf16[256,128]{1,0:T(8,128)(2,1)S(1)}, bf16[256,128]{1,0:T(8,128)(2,1)}, u32[]{:S(2)}) copy-start(bf16[256,128]{1,0:T(8,128)(2,1)} %param.10) | copy-start | bytes 196612
  45.5 10.7 %copy-start.7 = (s32[16]{0:T(128)S(1)}, s32[16]{0:T(128)}, u32[]{:S(2)}) copy-start(s32[16]{0:T(128)} %param.13) | copy-start | bytes 196
  54.1 3.4 %copy-start.3 = (f32[720,128]{1,0:T(8,128)S(1)}, f32[720,128]{1,0:T(8,128)}, u32[]{:S(2)}) copy-start(f32[720,128]{1,0:T(8,128)} %param.12) | copy-start | bytes 1105924
  106.1 12.6 %collective-permute-start.4 = (bf16[2,1,720,128]{3,2,1,0:T(8,128)(2,1)S(1)}, bf16[2,1,720,128]{3,2,1,0:T(8,128)(2,1)S(1)}, u32[]{:S(2)}, u32[]{:S(2)}) collective-permute-start(bf16[2,1,720,128]{3,2,1,0:T(8,128)(2,1)S(1)} %get-tuple-element.5), channel_id=1, source_target_pairs={{0,8},{8,16},{16,24},{24,32},{32,40},{40,48},{48,56},{56,64},{64,7... | collective-permute-start | bytes 1105928 | tf_op jit(solution)/shard_map/ppermute | solution.py:16
  109.3 14.5 %collective-permute-start.5 = (bf16[2,1,720,128]{3,2,1,0:T(8,128)(2,1)S(1)}, bf16[2,1,720,128]{3,2,1,0:T(8,128)(2,1)S(1)}, u32[]{:S(2)}, u32[]{:S(2)}) collective-permute-start(bf16[2,1,720,128]{3,2,1,0:T(8,128)(2,1)S(1)} %get-tuple-element.6), channel_id=1, source_target_pairs={{8,0},{16,8},{24,16},{32,24},{40,32},{48,40},{56,48},{64,56},{72,6... | collective-permute-start | bytes 1105928 | tf_op jit(solution)/shard_map/ppermute | solution.py:17
  157.7 4.6 %copy-start.6 = (bf16[3,3,128,128]{3,2,1,0:T(8,128)(2,1)S(1)}, bf16[3,3,128,128]{3,2,1,0:T(8,128)(2,1)}, u32[]{:S(2)}) copy-start(bf16[3,3,128,128]{3,2,1,0:T(8,128)(2,1)} %param.14) | copy-start | bytes 884740
  157.7 4.6 %copy-start.8 = (pred[16,91]{0,1:T(8,128)(4,1)S(1)}, pred[16,91]{0,1:T(8,128)(4,1)}, u32[]{:S(2)}) copy-start(pred[16,91]{0,1:T(8,128)(4,1)} %constant.37) | copy-start | bytes 4372
  188.7 11.6 %copy-start.5 = (bf16[720,720]{1,0:T(8,128)(2,1)S(1)}, bf16[720,720]{1,0:T(8,128)(2,1)}, u32[]{:S(2)}) copy-start(bf16[720,720]{1,0:T(8,128)(2,1)} %param.15) | copy-start | bytes 3110404
  200.3 12.3 %copy-start.1 = (bf16[3,3,256,256]{3,2,1,0:T(8,128)(2,1)S(1)}, bf16[3,3,256,256]{3,2,1,0:T(8,128)(2,1)}, u32[]{:S(2)}) copy-start(bf16[3,3,256,256]{3,2,1,0:T(8,128)(2,1)} %param.9) | copy-start | bytes 3538948
Sparse Core Ops, SparseCore 0:
  56.3 35.2 all-gather.1
where the time goes:
time: 223 us; the launch traced here: 220 us
  waiting for transfers between devices  49.1 us (22%)
  other arithmetic  47.8 us (21%)
  local copies, waits for them, and re-layouts  47 us (21%)
  matrix products  45 us (20%)
  starting transfers between devices  16.9 us (8%)
  between operations  13.9 us (6%)
    all_gather x1, waiting for transfers between devices, shards(): lax.all_gather(flat.astype(jnp.bfloat16).reshape(pooled.shape[0], pooled....  33.8 us
    conv_general_dilated x2, matrix products, conv_three(): lax.conv_general_dilated(batched, weight, (1, 1), 'VALID', dimension_numb...  30.8 us
    conv_general_dilated x5, local copies, waits for them, and re-layouts, conv_three(): lax.conv_general_dilated(batched, weight, (1, 1), 'VALID', dimension_numb...  17.9 us
    convert_element_type x2, local copies, waits for them, and re-layouts, shards(): hidden = jax.nn.gelu(conv_three(padded_head, w_head)).astype(jnp.bfloat16)  16.7 us
    concatenate x1, other arithmetic, wrap_columns(): jnp.concatenate([field[..., -1:, :], field, field[..., :1, :]], axis=-2)  13 us
    dot_general x1, matrix products, shards(): jnp.einsum('ij,bajc->baic', zonal_mix, hidden, preferred_element_type=jnp...  12.3 us
    ppermute x3, waiting for transfers between devices, extended(): before = lax.ppermute(last, axis, up)  9.7 us
    ppermute x3, starting transfers between devices, extended(): before = lax.ppermute(last, axis, up)  8.78 us
  transfers between devices with their start and end apart: 7, of which 6 were waited for; matrix products, arithmetic and copies ran while one was open for 1% of the time, Pallas kernels for 0%

commit v1 on v0

--- a/solution.py
+++ b/solution.py
@@ -60,11 +60,11 @@
     lon_group = lax.axis_index("lon")
     my_rows = lax.dynamic_slice_in_dim(lead_ids, lon_group * LEAD_DEV, LEAD_DEV)
     flat = jnp.dot(pooled.reshape(-1, channels), w_proj, preferred_element_type=jnp.float32)
-    band_proj = lax.all_gather(
-        flat.astype(jnp.bfloat16).reshape(pooled.shape[0], pooled.shape[1], head_width),
-        "lon",
-        axis=1,
-        tiled=True,
+    array = flat.astype(jnp.bfloat16).reshape(pooled.shape[0], pooled.shape[1], head_width)
+    peers = lax.axis_size("lon")
+    repeats = [peers if d == 1 else 1 for d in range(array.ndim)]
+    band_proj = lax.all_to_all(
+        jnp.tile(array, repeats), "lon", split_axis=1, concat_axis=1, tiled=True
     )
     onehot = (my_rows[:, None] == jnp.arange(film_scale.shape[0], dtype=jnp.int32)[None, :]).astype(
         jnp.float32

time: 223 us -> 236 us (1.058)
  waiting for transfers between devices: 49.1 us -> 67 us
  between operations: 13.9 us -> 0.58 us
  starting transfers between devices: 16.9 us -> 24 us
    all_to_all x0 -> x1, waiting for transfers between devices: none -> 51.5 us  [shards(): lax.all_to_all(jnp.tile(array, repeats), 'lon', split_axis=1, concat_axis...]
    all_gather x1 -> x0, waiting for transfers between devices: 33.8 us -> none  [shards(): lax.all_gather(flat.astype(jnp.bfloat16).reshape(pooled.shape[0], pooled....]
    all_to_all x0 -> x1, starting transfers between devices: none -> 4.58 us  [shards(): lax.all_to_all(jnp.tile(array, repeats), 'lon', split_axis=1, concat_axis...]
    ppermute x3, starting transfers between devices: 8.78 us -> 12.1 us  [extended(): before = lax.ppermute(last, axis, up)]
    another operation x0 -> x2, local copies, waits for them, and re-layouts: none -> 2.78 us  [shards(): jnp.tile(array, repeats)]
  transfers between devices with their start and end apart: 7 -> 7, of which waited for: 6 -> 6; matrix products, arithmetic and copies ran while one was open for 1% -> 0% of each run, Pallas kernels for 0% -> 0%
where the time goes in v1:
time: 236 us; the launch traced here: 232 us
  waiting for transfers between devices  67 us (28%)
  local copies, waits for them, and re-layouts  48.9 us (21%)
  other arithmetic  47.8 us (20%)
  matrix products  44 us (19%)
  starting transfers between devices  24 us (10%)
    all_to_all x1, waiting for transfers between devices, shards(): lax.all_to_all(jnp.tile(array, repeats), 'lon', split_axis=1, concat_axis...  51.5 us
    conv_general_dilated x2, matrix products, conv_three(): lax.conv_general_dilated(batched, weight, (1, 1), 'VALID', dimension_numb...  30.8 us
    conv_general_dilated x5, local copies, waits for them, and re-layouts, conv_three(): lax.conv_general_dilated(batched, weight, (1, 1), 'VALID', dimension_numb...  17.9 us
    convert_element_type x2, local copies, waits for them, and re-layouts, shards(): hidden = jax.nn.gelu(conv_three(padded_head, w_head)).astype(jnp.bfloat16)  16.7 us
    concatenate x1, other arithmetic, wrap_columns(): jnp.concatenate([field[..., -1:, :], field, field[..., :1, :]], axis=-2)  13 us
    dot_general x1, matrix products, shards(): jnp.einsum('ij,bajc->baic', zonal_mix, hidden, preferred_element_type=jnp...  12.3 us
    ppermute x3, starting transfers between devices, extended(): before = lax.ppermute(last, axis, up)  12.1 us
    ppermute x3, waiting for transfers between devices, extended(): before = lax.ppermute(last, axis, up)  8.62 us
  transfers between devices with their start and end apart: 7, of which 6 were waited for; matrix products, arithmetic and copies ran while one was open for 0% of the time, Pallas kernels for 0%

profile of v1, /device:TPU:96, one launch (start us, length us, event | category | flops | bytes accessed | tf_op | source)
XLA Modules:
  0.0 232.2 jit_solution(11235330423257330032)
XLA Ops:
  1.8 2.4 %collective-permute-start.1 = (bf16[1,180,256]{2,1,0:T(8,128)(2,1)S(1)}, bf16[1,180,256]{2,1,0:T(8,128)(2,1)S(1)}, u32[]{:S(2)}, u32[]{:S(2)}) collective-permute-start(bf16[1,180,256]{2,1,0:T(8,128)(2,1)S(1)} %copy.65), channel_id=1, source_target_pairs={{8,0},{16,8},{24,16},{32,24},{40,32},{48,40},{56,48},{64,56},{72,6... | collective-permute-start | bytes 276488 | tf_op jit(solution)/shard_map/ppermute | solution.py:17
  4.3 5.6 %collective-permute-start = (bf16[1,180,256]{2,1,0:T(8,128)(2,1)S(1)}, bf16[1,180,256]{2,1,0:T(8,128)(2,1)S(1)}, u32[]{:S(2)}, u32[]{:S(2)}) collective-permute-start(bf16[1,180,256]{2,1,0:T(8,128)(2,1)S(1)} %copy.64), channel_id=1, source_target_pairs={{0,8},{8,16},{16,24},{24,32},{32,40},{40,48},{48,56},{56,64},{64,7... | collective-permute-start | bytes 276488 | tf_op jit(solution)/shard_map/ppermute | solution.py:16
  13.0 2.9 %collective-permute-start.3 = (bf16[42,1,256]{2,0,1:T(8,128)(2,1)S(1)}, bf16[42,1,256]{2,0,1:T(8,128)(2,1)S(1)}, u32[]{:S(2)}, u32[]{:S(2)}) collective-permute-start(bf16[42,1,256]{2,0,1:T(8,128)(2,1)S(1)} %get-tuple-element.8), channel_id=1, source_target_pairs={{1,0},{2,1},{3,2},{4,3},{5,4},{6,5},{7,6},{0,7},{9,8},{10,9},{11,1... | collective-permute-start | bytes 64520 | tf_op jit(solution)/shard_map/ppermute | solution.py:17
  17.5 3.2 %maximum_bitcast_fusion = bf16[42,1,182,256]{3,0,2,1:T(8,128)(2,1)S(1)} fusion(bf16[42,1,256]{2,0,1:T(8,128)(2,1)S(1)} %collective-permute-done.3, bf16[1,180,256]{2,0,1:T(2,128)(2,1)S(1)} %copy.46, bf16[40,180,256]{2,0,1:T(8,128)(2,1)S(1)} %copy-done.2, bf16[1,180,256]{2,0,1:T(2,128)(2,1)S(1)} %copy.45, bf16[42,1,256]{2,0,1:T(8,128)(2,1)S(1)} %collective-permute-done.2), kind=kLoop, calls=%fused_computation.37 | loop fusion | flops 19568640 | bytes 7827456 | tf_op jit(solution)/shard_map/broadcast_in_dim | solution.py:23
  22.7 9.5 %broadcast_select_fusion = f32[40,8,23,256]{3,1,2,0:T(8,128)S(1)} fusion(pred[8,23]{0,1:T(8,128)(4,1)S(1)} %copy-done.10, bf16[3,3,256,256]{3,2,1,0:T(8,128)(2,1)S(1)} %copy-done, bf16[42,1,7,2,256]{4,2,3,0,1:T(8,128)(2,1)S(1)} %slice.36, bf16[42,1,8,23,256]{4,2,3,0,1:T(8,128)(2,1)S(1)} %copy.49), kind=kOutput, calls=%fused_computation.44 | convolution fusion | flops 8696995840 | bytes 12974264 | tf_op jit(solution)/shard_map/conv_general_dilated | solution.py:24
  32.2 2.6 %copy.50 = f32[40,8,23,256]{3,0,2,1:T(8,128)S(1)} copy(f32[40,8,23,256]{3,1,2,0:T(8,128)S(1)} %broadcast_select_fusion) | data formatting | bytes 15073280 | tf_op jit(solution)/shard_map/conv_general_dilated | solution.py:24
  34.8 4.2 %fusion.23 = f32[40,180,256]{2,0,1:T(8,128)} fusion(f32[40,1,184,256]{3,0,2,1:T(8,128)S(1)} %bitcast.43), kind=kLoop, calls=%fused_computation.33 | loop fusion | flops 14745600 | bytes 14745600 | tf_op jit(solution)/shard_map/mul | solution.py:57
  39.0 8.4 %reduce_window.7 = f32[20,90,256]{2,0,1:T(8,128)S(1)} reduce-window(f32[40,180,256]{2,0,1:T(8,128)} %fusion.23, f32[]{:T(128)} %constant.14.clone.1), window={size=2x2x1 stride=2x2x1}, to_apply=%region_0.0 | reduce-window | flops 1382400 | bytes 9216004 | tf_op jit(solution)/shard_map/reduce_window | solution.py:36
  48.8 2.7 %tile.11.clone = bf16[20,8,90,128]{3,0,2,1:T(8,128)(2,1)} broadcast(bf16[20,90,128]{2,0,1:T(8,128)(2,1)S(1)} %copy.67), dimensions={0,2,3} | broadcast | bytes 4147200 | tf_op jit(solution)/shard_map/tile | solution.py:67
  51.5 4.6 %all-to-all-start = ((bf16[20,720,128]{2,0,1:T(8,128)(2,1)}), bf16[20,720,128]{2,0,1:T(8,128)(2,1)}, u32[]{:S(2)}, u32[]{:S(2)}) async-start(bf16[20,720,128]{2,0,1:T(8,128)(2,1)} %bitcast.45), calls=%async_computation | async-start | bytes 8847360 | tf_op jit(solution)/shard_map/all_to_all | solution.py:66
  56.7 51.5 %all-to-all-done = bf16[20,720,128]{2,0,1:T(8,128)(2,1)} async-done(((bf16[20,720,128]{2,0,1:T(8,128)(2,1)}), bf16[20,720,128]{2,0,1:T(8,128)(2,1)}, u32[]{:S(2)}, u32[]{:S(2)}) %all-to-all-start) | async-done | bytes 3686432 | tf_op jit(solution)/shard_map/all_to_all | solution.py:66
  108.2 5.8 %copy_convert_fusion = f32[20,720,128]{2,1,0:T(8,128)} fusion(bf16[20,720,128]{2,0,1:T(8,128)(2,1)} %all-to-all-done), kind=kLoop, calls=%fused_computation.45 | loop fusion | flops 1843200 | bytes 11059200 | tf_op jit(solution)/shard_map/convert_element_type | solution.py:47
  114.0 7.6 %add_convert_fusion = bf16[2,20,720,128]{3,2,1,0:T(8,128)(2,1)} fusion(f32[2,128]{1,0:T(2,128)S(1)} %fusion.36, f32[2,128]{1,0:T(2,128)S(1)} %convolution_add_fusion, f32[20,720,128]{2,1,0:T(8,128)} %copy_convert_fusion), kind=kLoop, calls=%fused_computation.13 | loop fusion | flops 11059200 | bytes 14747648 | tf_op jit(solution)/shard_map/convert_element_type | solution.py:48
  122.8 6.4 %collective-permute-start.4 = (bf16[2,1,720,128]{3,2,1,0:T(8,128)(2,1)S(1)}, bf16[2,1,720,128]{3,2,1,0:T(8,128)(2,1)S(1)}, u32[]{:S(2)}, u32[]{:S(2)}) collective-permute-start(bf16[2,1,720,128]{3,2,1,0:T(8,128)(2,1)S(1)} %get-tuple-element.5), channel_id=1, source_target_pairs={{0,8},{8,16},{16,24},{24,32},{32,40},{40,48},{48,56},{56,64},{64,7... | collective-permute-start | bytes 1105928 | tf_op jit(solution)/shard_map/ppermute | solution.py:16
  131.1 5.7 %collective-permute-done.4 = bf16[2,1,720,128]{3,2,1,0:T(8,128)(2,1)S(1)} collective-permute-done((bf16[2,1,720,128]{3,2,1,0:T(8,128)(2,1)S(1)}, bf16[2,1,720,128]{3,2,1,0:T(8,128)(2,1)S(1)}, u32[]{:S(2)}, u32[]{:S(2)}) %collective-permute-start.4) | collective-permute-done | bytes 368672 | tf_op jit(solution)/shard_map/ppermute | solution.py:16
  136.8 6.2 %collective-permute-done.5 = bf16[2,1,720,128]{3,2,1,0:T(8,128)(2,1)S(1)} collective-permute-done((bf16[2,1,720,128]{3,2,1,0:T(8,128)(2,1)S(1)}, bf16[2,1,720,128]{3,2,1,0:T(8,128)(2,1)S(1)}, u32[]{:S(2)}, u32[]{:S(2)}) %collective-permute-start.5) | collective-permute-done | bytes 368672 | tf_op jit(solution)/shard_map/ppermute | solution.py:17
  143.1 13.0 %fusion.15 = bf16[22,2,722,128]{3,2,0,1:T(8,128)(2,1)} fusion(bf16[2,1,720,128]{3,2,1,0:T(8,128)(2,1)S(1)} %collective-permute-done.5, bf16[2,20,720,128]{3,2,1,0:T(8,128)(2,1)} %add_convert_fusion, bf16[2,1,720,128]{3,2,1,0:T(8,128)(2,1)S(1)} %collective-permute-done.4), kind=kLoop, calls=%fused_computation.22 | loop fusion | flops 73193472 | bytes 16242688 | tf_op jit(solution)/shard_map/concatenate | solution.py:43
  156.1 7.0 %pad.2 = bf16[22,2,728,128]{3,2,0,1:T(8,128)(2,1)} pad(bf16[22,2,722,128]{3,2,0,1:T(8,128)(2,1)} %fusion.15, bf16[]{:T(256)} %constant.6), padding=0_0x0_0x0_6x0_0 | pad | bytes 16332802 | tf_op jit(solution)/shard_map/concatenate | solution.py:43
  163.1 12.6 %reshape.39 = bf16[22,2,8,91,128]{4,3,2,0,1:T(8,128)(2,1)} reshape(bf16[22,2,728,128]{3,2,0,1:T(8,128)(2,1)} %pad.2) | data formatting | bytes 16400384 | tf_op jit(solution)/shard_map/conv_general_dilated | solution.py:24
  177.0 4.6 %fusion.10 = bf16[22,2,8,93,128]{4,3,2,1,0:T(8,128)(2,1)S(1)} fusion(bf16[22,2,7,2,128]{4,3,2,1,0:T(2,128)(2,1)S(1)} %copy.79, bf16[22,2,8,91,128]{4,3,2,0,1:T(8,128)(2,1)} %reshape.39), kind=kLoop, calls=%fused_computation.15 | loop fusion | flops 25141248 | bytes 16738304 | tf_op jit(solution)/shard_map/conv_general_dilated | solution.py:24
  181.7 21.3 %fusion.8 = bf16[20,16,91,128]{3,1,2,0:T(8,128)(2,1)S(1)} fusion(bf16[3,3,128,128]{3,2,1,0:T(8,128)(2,1)S(1)} %copy-done.7, bf16[22,2,8,93,128]{4,3,2,1,0:T(8,128)(2,1)S(1)} %fusion.10, pred[16,91]{0,1:T(8,128)(4,1)S(1)} %copy-done.9), kind=kOutput, calls=%fused_computation.10 | convolution fusion | flops 8625111040 | bytes 16131504 | tf_op jit(solution)/shard_map/conv_general_dilated | solution.py:24
  203.0 5.1 %copy.56 = bf16[20,16,91,128]{3,2,1,0:T(8,128)(2,1)} copy(bf16[20,16,91,128]{3,1,2,0:T(8,128)(2,1)S(1)} %fusion.8) | data formatting | bytes 14909440 | tf_op jit(solution)/shard_map/convert_element_type | solution.py:79
  208.0 11.6 %reshape.27 = bf16[20,2,728,128]{3,2,1,0:T(8,128)(2,1)} reshape(bf16[20,16,91,128]{3,2,1,0:T(8,128)(2,1)} %copy.56) | data formatting | bytes 14909440 | tf_op jit(solution)/shard_map/convert_element_type | solution.py:79
  219.6 12.3 %fusion.9 = bf16[2,20,720,128]{3,2,1,0:T(8,128)(2,1)} fusion(bf16[2,20,720,128]{3,2,1,0:T(8,128)(2,1)} %add_convert_fusion, bf16[720,720]{1,0:T(8,128)(2,1)S(1)} %copy-done.6, bf16[20,2,728,128]{3,2,1,0:T(8,128)(2,1)} %reshape.27), kind=kOutput, calls=%fused_computation.12 | convolution fusion | flops 5319475200 | bytes 23155200 | tf_op jit(solution)/shard_map/ij,bajc->baic/dot_general | solution.py:80
  (49 shorter events, 14.8 us)
Async XLA Ops:
  0.0 22.7 %copy-start = (bf16[3,3,256,256]{3,2,1,0:T(8,128)(2,1)S(1)}, bf16[3,3,256,256]{3,2,1,0:T(8,128)(2,1)}, u32[]{:S(2)}) copy-start(bf16[3,3,256,256]{3,2,1,0:T(8,128)(2,1)} %param.9) | copy-start | bytes 3538948
  0.0 17.5 %copy-start.2 = (bf16[40,180,256]{2,0,1:T(8,128)(2,1)S(1)}, bf16[40,180,256]{2,0,1:T(8,128)(2,1)}, u32[]{:S(2)}) copy-start(bf16[40,180,256]{2,0,1:T(8,128)(2,1)} %param.8) | copy-start | bytes 11059204
  1.8 8.7 %collective-permute-start.1 = (bf16[1,180,256]{2,1,0:T(8,128)(2,1)S(1)}, bf16[1,180,256]{2,1,0:T(8,128)(2,1)S(1)}, u32[]{:S(2)}, u32[]{:S(2)}) collective-permute-start(bf16[1,180,256]{2,1,0:T(8,128)(2,1)S(1)} %copy.65), channel_id=1, source_target_pairs={{8,0},{16,8},{24,16},{32,24},{40,32},{48,40},{56,48},{64,56},{72,6... | collective-permute-start | bytes 276488 | tf_op jit(solution)/shard_map/ppermute | solution.py:17
  4.3 7.8 %collective-permute-start = (bf16[1,180,256]{2,1,0:T(8,128)(2,1)S(1)}, bf16[1,180,256]{2,1,0:T(8,128)(2,1)S(1)}, u32[]{:S(2)}, u32[]{:S(2)}) collective-permute-start(bf16[1,180,256]{2,1,0:T(8,128)(2,1)S(1)} %copy.64), channel_id=1, source_target_pairs={{0,8},{8,16},{16,24},{24,32},{32,40},{40,48},{48,56},{56,64},{64,7... | collective-permute-start | bytes 276488 | tf_op jit(solution)/shard_map/ppermute | solution.py:16
  13.0 4.5 %collective-permute-start.2 = (bf16[42,1,256]{2,0,1:T(8,128)(2,1)S(1)}, bf16[42,1,256]{2,0,1:T(8,128)(2,1)S(1)}, u32[]{:S(2)}, u32[]{:S(2)}) collective-permute-start(bf16[42,1,256]{2,0,1:T(8,128)(2,1)S(1)} %get-tuple-element.7), channel_id=1, source_target_pairs={{0,1},{1,2},{2,3},{3,4},{4,5},{5,6},{6,7},{7,0},{8,9},{9,10},{10,1... | collective-permute-start | bytes 64520 | tf_op jit(solution)/shard_map/ppermute | solution.py:16
  13.0 4.5 %collective-permute-start.3 = (bf16[42,1,256]{2,0,1:T(8,128)(2,1)S(1)}, bf16[42,1,256]{2,0,1:T(8,128)(2,1)S(1)}, u32[]{:S(2)}, u32[]{:S(2)}) collective-permute-start(bf16[42,1,256]{2,0,1:T(8,128)(2,1)S(1)} %get-tuple-element.8), channel_id=1, source_target_pairs={{1,0},{2,1},{3,2},{4,3},{5,4},{6,5},{7,6},{0,7},{9,8},{10,9},{11,1... | collective-permute-start | bytes 64520 | tf_op jit(solution)/shard_map/ppermute | solution.py:17
  20.7 2.0 copy-start.10
  39.0 9.1 %copy-start.5 = (bf16[256,128]{1,0:T(8,128)(2,1)S(1)}, bf16[256,128]{1,0:T(8,128)(2,1)}, u32[]{:S(2)}) copy-start(bf16[256,128]{1,0:T(8,128)(2,1)} %param.10) | copy-start | bytes 196612
  48.5 7.6 %copy-start.8 = (s32[16]{0:T(128)S(1)}, s32[16]{0:T(128)}, u32[]{:S(2)}) copy-start(s32[16]{0:T(128)} %param.13) | copy-start | bytes 196
  48.5 7.7 %copy-start.3 = (f32[720,128]{1,0:T(8,128)S(1)}, f32[720,128]{1,0:T(8,128)}, u32[]{:S(2)}) copy-start(f32[720,128]{1,0:T(8,128)} %param.11) | copy-start | bytes 1105924
  48.5 7.9 %copy-start.4 = (f32[720,128]{1,0:T(8,128)S(1)}, f32[720,128]{1,0:T(8,128)}, u32[]{:S(2)}) copy-start(f32[720,128]{1,0:T(8,128)} %param.12) | copy-start | bytes 1105924
  51.5 56.7 %all-to-all-start = ((bf16[20,720,128]{2,0,1:T(8,128)(2,1)}), bf16[20,720,128]{2,0,1:T(8,128)(2,1)}, u32[]{:S(2)}, u32[]{:S(2)}) async-start(bf16[20,720,128]{2,0,1:T(8,128)(2,1)} %bitcast.45), calls=%async_computation | async-start | bytes 8847360 | tf_op jit(solution)/shard_map/all_to_all | solution.py:66
  122.8 14.1 %collective-permute-start.4 = (bf16[2,1,720,128]{3,2,1,0:T(8,128)(2,1)S(1)}, bf16[2,1,720,128]{3,2,1,0:T(8,128)(2,1)S(1)}, u32[]{:S(2)}, u32[]{:S(2)}) collective-permute-start(bf16[2,1,720,128]{3,2,1,0:T(8,128)(2,1)S(1)} %get-tuple-element.5), channel_id=1, source_target_pairs={{0,8},{8,16},{16,24},{24,32},{32,40},{40,48},{48,56},{56,64},{64,7... | collective-permute-start | bytes 1105928 | tf_op jit(solution)/shard_map/ppermute | solution.py:16
  129.2 13.9 %collective-permute-start.5 = (bf16[2,1,720,128]{3,2,1,0:T(8,128)(2,1)S(1)}, bf16[2,1,720,128]{3,2,1,0:T(8,128)(2,1)S(1)}, u32[]{:S(2)}, u32[]{:S(2)}) collective-permute-start(bf16[2,1,720,128]{3,2,1,0:T(8,128)(2,1)S(1)} %get-tuple-element.6), channel_id=1, source_target_pairs={{8,0},{16,8},{24,16},{32,24},{40,32},{48,40},{56,48},{64,56},{72,6... | collective-permute-start | bytes 1105928 | tf_op jit(solution)/shard_map/ppermute | solution.py:17
  177.0 4.6 %copy-start.7 = (bf16[3,3,128,128]{3,2,1,0:T(8,128)(2,1)S(1)}, bf16[3,3,128,128]{3,2,1,0:T(8,128)(2,1)}, u32[]{:S(2)}) copy-start(bf16[3,3,128,128]{3,2,1,0:T(8,128)(2,1)} %param.14) | copy-start | bytes 884740
  177.0 4.6 %copy-start.9 = (pred[16,91]{0,1:T(8,128)(4,1)S(1)}, pred[16,91]{0,1:T(8,128)(4,1)}, u32[]{:S(2)}) copy-start(pred[16,91]{0,1:T(8,128)(4,1)} %constant.37) | copy-start | bytes 4372
  208.0 11.6 %copy-start.6 = (bf16[720,720]{1,0:T(8,128)(2,1)S(1)}, bf16[720,720]{1,0:T(8,128)(2,1)}, u32[]{:S(2)}) copy-start(bf16[720,720]{1,0:T(8,128)(2,1)} %param.15) | copy-start | bytes 3110404
  219.6 12.3 %copy-start.1 = (bf16[3,3,256,256]{3,2,1,0:T(8,128)(2,1)S(1)}, bf16[3,3,256,256]{3,2,1,0:T(8,128)(2,1)}, u32[]{:S(2)}) copy-start(bf16[3,3,256,256]{3,2,1,0:T(8,128)(2,1)} %param.9) | copy-start | bytes 3538948
